TPU v7x, 512 devices: a whole 4x8x8 slice. The times are simulated.
512 devices in a mesh: grp: 8 (over y), sp: 64 (over x, z, core).
Axes of the slice: x: 4, y: 8, z: 8, core: 2. Of those that a mesh axis runs over, the one named last changes fastest.
Arguments:
- snapshots: float32 [3, 8192, 24576], P(None, 'grp', 'sp'), may hold values from -12 to 12
- kept_bins: int32 [64], replicated, may hold values from 1 to 255, as said below
- weights: float32 [24576], P('sp'), may hold values from 0.1 to 80
Outputs:
- mode_fields: float32 [2, 64, 4, 3, 24576], P(None, 'grp', None, None, 'sp')
- energies: float32 [64, 4], P('grp')
Inputs may be any that keep to these rules, and one draw needn't show every extreme that they name: `kept_bins`: 64 distinct bins in increasing order; both 1 and 255 are among them.
All inputs are finite; a program needn't handle non-finite values.
Results may differ from a plain program's by a relative error of at most 0.0003.
Values sent between devices are 32-bit elements; how exact they have to be, the bound alone decides.
A program may use at most 64 MiB of HBM per device.

v0:
```python
import math

import jax
import jax.numpy as jnp
from jax import lax
from jax.sharding import PartitionSpec as P

L = 512
HOP = 256
MODES = 4
ITERS = 3


precise = lax.Precision.HIGHEST


def make_table(kept_bins, block_len):
    offsets = jnp.arange(block_len, dtype=jnp.int32)
    phases = kept_bins[:, None] * offsets[None, :] % block_len
    angles = phases.astype(jnp.float32) * (2.0 * math.pi / block_len)
    window = (
        0.5 - 0.5 * jnp.cos(offsets.astype(jnp.float32) * (2.0 * math.pi / block_len))
    ) / math.sqrt(3.0 * block_len / 8.0)
    return jnp.stack([window * jnp.cos(angles), -window * jnp.sin(angles)])


def orthonormalize(w_real, w_imag):
    basis_re = []
    basis_im = []
    lengths = []
    for column in range(w_real.shape[-1]):
        orig_re = w_real[..., column]
        orig_im = w_imag[..., column]
        left_re = orig_re
        left_im = orig_im
        for earlier in range(column):
            prev_re = basis_re[earlier]
            prev_im = basis_im[earlier]
            coef_re = jnp.sum(prev_re * orig_re + prev_im * orig_im, axis=-1, keepdims=True)
            coef_im = jnp.sum(prev_re * orig_im - prev_im * orig_re, axis=-1, keepdims=True)
            left_re = left_re - (coef_re * prev_re - coef_im * prev_im)
            left_im = left_im - (coef_re * prev_im + coef_im * prev_re)
        length = jnp.sqrt(jnp.sum(left_re * left_re + left_im * left_im, axis=-1) + 1e-06)
        basis_re.append(left_re / length[..., None])
        basis_im.append(left_im / length[..., None])
        lengths.append(length)
    return (jnp.stack(basis_re, -1), jnp.stack(basis_im, -1), jnp.stack(lengths, -1))


def apply_gram(gram_re, gram_im, v_real, v_imag):
    pattern = "fbd,fdm->fbm"
    out_re = jnp.einsum(pattern, gram_re, v_real, precision=precise) - jnp.einsum(
        pattern, gram_im, v_imag, precision=precise
    )
    out_im = jnp.einsum(pattern, gram_re, v_imag, precision=precise) + jnp.einsum(
        pattern, gram_im, v_real, precision=precise
    )
    return (out_re, out_im)


def subspace(apply_fn, freq_count, block_count, mode_count):
    identity_cols = jnp.eye(block_count, mode_count, dtype=jnp.float32)
    v_real = jnp.broadcast_to(identity_cols, (freq_count, block_count, mode_count))
    v_imag = jnp.zeros((freq_count, block_count, mode_count), jnp.float32)
    lengths = jnp.zeros((freq_count, mode_count), jnp.float32)
    for sweep_step in range(ITERS):
        w_real, w_imag = apply_fn(v_real, v_imag)
        v_real, v_imag, lengths = orthonormalize(w_real, w_imag)
    return (v_real, v_imag, lengths)


def local_gram(x_real, x_imag, point_wts, norm_factor):
    y_real = x_real * point_wts
    y_imag = x_imag * point_wts
    pattern = "bfcp,dfcp->fbd"
    g_re = (
        jnp.einsum(pattern, y_real, x_real, precision=precise)
        + jnp.einsum(pattern, y_imag, x_imag, precision=precise)
    ) * norm_factor
    g_im = (
        jnp.einsum(pattern, y_real, x_imag, precision=precise)
        - jnp.einsum(pattern, y_imag, x_real, precision=precise)
    ) * norm_factor
    return (g_re, g_im)


def form_modes(x_real, x_imag, v_real, v_imag, lengths, block_count):
    pattern = "bfcp,fbm->fmcp"
    m_re = jnp.einsum(pattern, x_real, v_real, precision=precise) - jnp.einsum(
        pattern, x_imag, v_imag, precision=precise
    )
    m_im = jnp.einsum(pattern, x_real, v_imag, precision=precise) + jnp.einsum(
        pattern, x_imag, v_real, precision=precise
    )
    factor = (1.0 / jnp.sqrt(block_count * lengths))[:, :, None, None]
    return jnp.stack([m_re * factor, m_im * factor])


def total_gram(gram_parts):
    return lax.psum((gram_parts[0], gram_parts[1]), "sp")


def shards(snapshots, kept_bins, weights):
    dft_table = make_table(kept_bins, L)
    local_points = weights.shape[0]
    block_local = snapshots.shape[1] // HOP
    block_count = block_local * lax.axis_size("grp")
    norm_factor = 1.0 / (3.0 * local_points * lax.axis_size("sp"))
    regrouped = lax.all_to_all(snapshots, "grp", split_axis=2, concat_axis=1, tiled=True)
    sub_points = regrouped.shape[2]
    segments = regrouped.reshape(3, block_count, HOP, sub_points)
    following = jnp.roll(segments, -1, axis=1)
    blocks = jnp.concatenate([segments, following], axis=2)
    spectra = jnp.einsum("kft,cbtp->bkfcp", dft_table, blocks, precision=precise)
    x_real = spectra[:, 0]
    x_imag = spectra[:, 1]
    sub_wts = lax.dynamic_slice_in_dim(weights, lax.axis_index("grp") * sub_points, sub_points)
    g_re, g_im = local_gram(x_real, x_imag, sub_wts, norm_factor)
    g_re, g_im = (
        lax.psum_scatter(g_re, "grp", scatter_dimension=0, tiled=True),
        lax.psum_scatter(g_im, "grp", scatter_dimension=0, tiled=True),
    )
    g_re, g_im = total_gram((g_re, g_im))
    freq_count = g_re.shape[0]

    def apply_fn(v_real, v_imag):
        return apply_gram(g_re, g_im, v_real, v_imag)

    v_real, v_imag, lengths = subspace(apply_fn, freq_count, block_count, MODES)
    all_re, all_im, all_len = (
        lax.all_gather(v_real, "grp", axis=0, tiled=True),
        lax.all_gather(v_imag, "grp", axis=0, tiled=True),
        lax.all_gather(lengths, "grp", axis=0, tiled=True),
    )
    mode_fields = form_modes(x_real, x_imag, all_re, all_im, all_len, block_count)
    mode_fields = lax.all_to_all(mode_fields, "grp", split_axis=1, concat_axis=4, tiled=True)
    return (mode_fields, lengths)


def solution(mesh):
    in_specs = (P(None, "grp", "sp"), P(), P("sp"))
    out_specs = (P(None, "grp", None, None, "sp"), P("grp", None))
    return jax.shard_map(shards, mesh=mesh, in_specs=in_specs, out_specs=out_specs, check_vma=False)
```

profile of v0, /device:TPU:2, one launch (start us, length us, event | category | flops | bytes accessed | tf_op | source)
XLA Modules:
  0.0 621.5 jit_solution(10956544655818458053)
XLA Ops:
  7.2 7.4 %copy.333 = f32[3,1024,384]{1,0,2:T(4,128)} copy(f32[3,1024,384]{2,1,0:T(8,128)} %param.3) | data formatting | bytes 9437184 | tf_op args[0]
  14.6 7.2 %all-to-all-start = ((f32[3,1024,384]{1,0,2:T(4,128)}), f32[3,1024,384]{1,0,2:T(4,128)}, u32[]{:S(2)}, u32[]{:S(2)}) async-start(f32[3,1024,384]{1,0,2:T(4,128)} %copy.333), calls=%async_computation | async-start | bytes 12582912 | tf_op jit(solution)/shard_map/all_to_all | solution.py:109
  23.3 140.1 %all-to-all-done = f32[3,1024,384]{1,0,2:T(4,128)} async-done(((f32[3,1024,384]{1,0,2:T(4,128)}), f32[3,1024,384]{1,0,2:T(4,128)}, u32[]{:S(2)}, u32[]{:S(2)}) %all-to-all-start) | async-done | bytes 4718624 | tf_op jit(solution)/shard_map/all_to_all | solution.py:109
  163.3 5.5 copy.334
  168.8 4.9 copy.335
  173.7 6.5 %reshape.1735 = f32[3,32,256,48]{2,1,3,0:T(8,128)} reshape(f32[3,8,1024,48]{2,1,3,0:T(8,128)} %copy.335) | data formatting | bytes 9437184 | tf_op jit(solution)/shard_map/reshape | solution.py:111
  180.2 5.1 copy.338
  185.7 7.6 %fusion.5 = f32[32,2,64,3,48]{2,4,1,0,3:T(8,128)S(1)} fusion(f32[3,1,256,48]{2,3,1,0:T(8,128)S(1)} %slice.115, f32[3,31,256,48]{2,3,1,0:T(8,128)S(1)} %slice.114, f32[3,32,256,48]{2,3,1,0:T(8,128)S(1)} %copy.338, f32[1,64,512]{2,1,0:T(8,128)S(1)} %get-tuple-element.104, f32[1,64,512]{2,1,0:T(8,128)S(1)} %get-tuple-element.103), kind=kOutput, calls=%fused_computation.8 | convolution fusion | flops 3628662784 | bytes 12058624 | tf_op jit(solution)/shard_map/kft,cbtp->bkfcp/dot_general | solution.py:114
  197.9 2.8 copy.343
  200.7 3.7 copy.340
  204.4 2.9 copy.341
  207.4 3.7 copy.342
  211.1 5.8 convolution_bitcast_fusion
  217.0 4.8 fusion.9
  222.3 6.8 %convolution_bitcast_fusion.2 = f32[64,32,32]{2,1,0:T(8,128)S(1)} fusion(f32[32,64,3,48]{3,0,2,1:T(8,128)} %copy.342, f32[32,64,3,48]{3,0,2,1:T(8,128)} %copy.343), kind=kOutput, calls=%fused_computation.11 | convolution fusion | flops 113246208 | bytes 2621440 | tf_op jit(solution)/shard_map/bfcp,dfcp->fbd/dot_general | solution.py:78
  229.1 4.8 fusion.7
  234.0 28.4 %reduce-scatter.5.cloned.1.call-done = f32[8,32,32]{2,1,0:T(8,128)} async-done(((f32[64,32,32]{2,1,0:T(8,128)}), f32[8,32,32]{2,1,0:T(8,128)}) %reduce-scatter.5.cloned.1.call-update) | async-done | bytes 32784 | tf_op jit(solution)/shard_map/reduce_scatter | solution.py:121
  262.4 43.0 %reduce-scatter.3.cloned.1.call-done = f32[8,32,32]{2,1,0:T(8,128)} async-done(((f32[64,32,32]{2,1,0:T(8,128)}), f32[8,32,32]{2,1,0:T(8,128)}) %reduce-scatter.3.cloned.1.call-update) | async-done | bytes 32784 | tf_op jit(solution)/shard_map/reduce_scatter | solution.py:120
  305.4 188.0 %all-reduce.3.cloned.1.call-done = (f32[8,32,32]{2,1,0:T(8,128)}, f32[8,32,32]{2,1,0:T(8,128)}) async-done(((f32[8,32,32]{2,1,0:T(8,128)}, f32[8,32,32]{2,1,0:T(8,128)}), (f32[8,32,32]{2,1,0:T(8,128)}, f32[8,32,32]{2,1,0:T(8,128)})) %all-reduce.3.cloned.1.call-update) | async-done | bytes 65552 | tf_op jit(solution)/shard_map/psum | solution.py:100
  513.2 23.7 %all-gather = f32[8,8,4]{1,2,0:T(4,128)S(1)} all-gather(f32[1,8,4]{1,2,0:T(4,128)S(1)} %fusion.200), channel_id=1, replica_groups=mesh['grp'=8,'sp'=64] {'grp'}, dimensions={0}, use_global_device_ids=true | all-gather | bytes 1152 | tf_op jit(solution)/shard_map/all_gather | solution.py:133
  537.0 24.6 %all_gather.10 = f32[64,32,4]{1,2,0:T(4,128)S(1)} all-gather(f32[8,32,4]{1,2,0:T(4,128)S(1)} %copy.370), channel_id=1, replica_groups=mesh['grp'=8,'sp'=64] {'grp'}, dimensions={0}, use_global_device_ids=true | all-gather | bytes 36864 | tf_op jit(solution)/shard_map/all_gather | solution.py:132
  561.6 24.7 %all_gather.9 = f32[64,32,4]{1,2,0:T(4,128)S(1)} all-gather(f32[8,32,4]{1,2,0:T(4,128)S(1)} %copy.368), channel_id=1, replica_groups=mesh['grp'=8,'sp'=64] {'grp'}, dimensions={0}, use_global_device_ids=true | all-gather | bytes 36864 | tf_op jit(solution)/shard_map/all_gather | solution.py:131
  595.8 3.9 all-to-all-start.1
  600.3 10.2 %all-to-all-done.1 = f32[8,1,9216]{2,1,0:T(1,128)S(1)} async-done(((f32[8,1,9216]{2,1,0:T(1,128)}), f32[8,1,9216]{2,1,0:T(1,128)S(1)}, u32[]{:S(2)}, u32[]{:S(2)}) %all-to-all-start.1) | async-done | bytes 294944 | tf_op jit(solution)/shard_map/all_to_all | solution.py:136
  (104 shorter events, 41.0 us)
Async XLA Ops:
  14.6 8.1 %copy-start.4 = (s32[64]{0:T(128)S(1)}, s32[64]{0:T(128)}, u32[]{:S(2)}) copy-start(s32[64]{0:T(128)} %param.4) | copy-start | bytes 772
  14.6 148.8 %all-to-all-start = ((f32[3,1024,384]{1,0,2:T(4,128)}), f32[3,1024,384]{1,0,2:T(4,128)}, u32[]{:S(2)}, u32[]{:S(2)}) async-start(f32[3,1024,384]{1,0,2:T(4,128)} %copy.333), calls=%async_computation | async-start | bytes 12582912 | tf_op jit(solution)/shard_map/all_to_all | solution.py:109
  21.8 240.6 %reduce-scatter.5.cloned.1.call-start = ((), (), s32[]{:S(2)}) async-start(), calls=%async_computation.5 | async-start | bytes 1179648 | tf_op jit(solution)/shard_map/reduce_scatter | solution.py:121
  211.1 5.9 copy-start
  211.1 5.9 copy-start.2
  221.8 83.6 %reduce-scatter.3.cloned.1.call-start = ((), (), s32[]{:S(2)}) async-start(), calls=%async_computation.4 | async-start | bytes 1179648 | tf_op jit(solution)/shard_map/reduce_scatter | solution.py:120
  222.3 6.8 %copy-start.3 = (f32[32,64,3,48]{3,0,2,1:T(8,128)S(1)}, f32[32,64,3,48]{3,0,2,1:T(8,128)}, u32[]{:S(2)}) copy-start(f32[32,64,3,48]{3,0,2,1:T(8,128)} %copy.340) | copy-start | bytes 3538948
  233.9 259.5 %all-reduce.3.cloned.1.call-start = ((), (), s32[]{:S(2)}) async-start(), calls=%async_computation.6 | async-start | bytes 524288 | tf_op jit(solution)/shard_map/psum | solution.py:100
  586.3 3.8 copy-start.1
  595.8 14.7 %all-to-all-start.1 = ((f32[8,1,9216]{2,1,0:T(1,128)}), f32[8,1,9216]{2,1,0:T(1,128)S(1)}, u32[]{:S(2)}, u32[]{:S(2)}) async-start(f32[8,1,9216]{2,1,0:T(1,128)} %reshape.1749), calls=%async_computation.3 | async-start | bytes 589824 | tf_op jit(solution)/shard_map/all_to_all | solution.py:136
Sparse Core Ops, SparseCore 0:
  221.9 40.4 reduce-scatter.4
  265.2 40.1 reduce-scatter.2
  308.9 184.4 all-reduce.2
where the time goes:
time: 628 us; the launch traced here: 622 us
  waiting for transfers between devices  410 us (65%)
  blocking collectives  73 us (12%)
  matrix products  52.3 us (8%)
  local copies, waits for them, and re-layouts  50.2 us (8%)
  between operations  14.3 us (2%)
  starting transfers between devices  11.7 us (2%)
  other arithmetic  10.3 us (2%)
    psum x1, waiting for transfers between devices, total_gram(): return lax.psum((gram_parts[0], gram_parts[1]), 'sp')  188 us
    all_to_all x1, waiting for transfers between devices, shards(): lax.all_to_all(snapshots, 'grp', split_axis=2, concat_axis=1, tiled=True)  140 us
    reduce_scatter x1, waiting for transfers between devices, shards(): lax.psum_scatter(g_re, 'grp', scatter_dimension=0, tiled=True)  43 us
    reduce_scatter x1, waiting for transfers between devices, shards(): lax.psum_scatter(g_im, 'grp', scatter_dimension=0, tiled=True)  28.4 us
    all_gather x1, blocking collectives, shards(): lax.all_gather(v_real, 'grp', axis=0, tiled=True)  24.7 us
    all_gather x1, blocking collectives, shards(): lax.all_gather(v_imag, 'grp', axis=0, tiled=True)  24.6 us
    all_gather x1, blocking collectives, shards(): lax.all_gather(lengths, 'grp', axis=0, tiled=True)  23.7 us
  transfers between devices with their start and end apart: 5, of which 5 were waited for; matrix products, arithmetic and copies ran while one was open for 2% of the time, Pallas kernels for 0%

commit v1 on v0

v1 whole, which is shorter than its diff:
```python
import functools
import math

import jax
import jax.numpy as jnp
from jax import lax
from jax.experimental import pallas as pl
from jax.experimental.pallas import tpu as pltpu
from jax.sharding import PartitionSpec as P

L = 512
HOP = 256
MODES = 4
ITERS = 3
GRP = 8
FPG = 8
RED = 8
ZS = 8
CORES = 2
NB = 4
NBLK = GRP * NB
MESH = pl.DeviceIdType.MESH


def cos_sin(phase):
    quarter = (phase + 64) >> 7
    rest = (phase - (quarter << 7)).astype(jnp.float32) * (2.0 * math.pi / L)
    sq = rest * rest
    sin = rest * (1.0 + sq * (-1.0 / 6 + sq * (1.0 / 120 + sq * (-1.0 / 5040 + sq * (1.0 / 362880)))))
    cos = 1.0 + sq * (-0.5 + sq * (1.0 / 24 + sq * (-1.0 / 720 + sq * (1.0 / 40320 - sq * (1.0 / 3628800)))))
    quarter = quarter & 3
    odd = (quarter & 1) == 1
    cos_q = jnp.where(odd, sin, cos)
    sin_q = jnp.where(odd, cos, sin)
    cos_q = jnp.where((quarter == 1) | (quarter == 2), -cos_q, cos_q)
    sin_q = jnp.where(quarter >= 2, -sin_q, sin_q)
    return cos_q, sin_q


def split(x):
    high = x.astype(jnp.bfloat16)
    low = (x - high.astype(jnp.float32)).astype(jnp.bfloat16)
    return high, low


def fdot(a, b):
    return jnp.dot(a, b, preferred_element_type=jnp.float32)


def make_tables(bins_ref, tab_hi, tab_lo):
    shape = (FPG, HOP)
    row = lax.broadcasted_iota(jnp.int32, shape, 0)
    time = lax.broadcasted_iota(jnp.int32, shape, 1)
    scale = 1.0 / math.sqrt(3.0 * L / 8.0)
    window = (0.5 - 0.5 * cos_sin(time)[0]) * scale
    second = scale - window
    for group in range(GRP):
        bins = jnp.full(shape, bins_ref[group * FPG], jnp.int32)
        for f in range(1, FPG):
            bins = jnp.where(row == f, bins_ref[group * FPG + f], bins)
        cos, sin = cos_sin((bins * time) & (L - 1))
        signed = jnp.where((bins & 1) == 1, -second, second)
        base = group * 2 * FPG
        for part, wave in ((0, cos), (1, -sin)):
            rows = pl.ds(base + part * FPG, FPG)
            for half, win in ((0, window), (1, signed)):
                high, low = split(wave * win)
                tab_hi[rows, half * HOP : (half + 1) * HOP] = high
                tab_lo[rows, half * HOP : (half + 1) * HOP] = low


def orthonormalize(w):
    lane = lax.broadcasted_iota(jnp.int32, w.shape, 1)
    lane_row = lax.broadcasted_iota(jnp.int32, (1, w.shape[1]), 1)
    w_re, w_im = w[:NBLK], w[NBLK:]
    left = w
    basis = jnp.zeros_like(w)
    lengths = jnp.ones((1, w.shape[1]), jnp.float32)
    for m in range(MODES):
        length = jnp.sqrt(jnp.sum(left * left, axis=0, keepdims=True) + 1e-06)
        unit = left / length
        basis = jnp.where(lane == m, unit, basis)
        lengths = jnp.where(lane_row == m, length, lengths)
        if m < MODES - 1:
            q = jnp.broadcast_to(unit[:, m : m + 1], w.shape)
            q_re, q_im = q[:NBLK], q[NBLK:]
            coef_re = jnp.sum(q_re * w_re + q_im * w_im, axis=0, keepdims=True)
            coef_im = jnp.sum(q_re * w_im - q_im * w_re, axis=0, keepdims=True)
            left = left - jnp.concatenate(
                [coef_re * q_re - coef_im * q_im, coef_re * q_im + coef_im * q_re], axis=0
            )
    return basis, lengths


def kernel(
    norm,
    bins_ref,
    wts_ref,
    snap_ref,
    modes_ref,
    en_ref,
    data,
    d_hi,
    d_lo,
    tab_hi,
    tab_lo,
    send,
    recv,
    hsend,
    hrecv,
    gram,
    gsend,
    rrecv,
    zpart,
    zrecv,
    vsend,
    vrecv,
    coef,
    in_sem,
    own_sem,
    h_ssem,
    h_rsem,
    a_ssem,
    a_rsem,
    r_ssem,
    r_rsem,
    z_ssem,
    z_rsem,
    v_ssem,
    v_rsem,
):
    comps = data.shape[0]
    points = data.shape[2]
    grp = lax.axis_index("grp")
    sp = lax.axis_index("sp")
    core = sp % CORES
    z = (sp // CORES) % ZS
    x = sp // (CORES * ZS)
    red = x * CORES + core

    def grp_peer(off):
        return (grp + off) % GRP, sp

    def red_peer(off):
        other = (red + off) % RED
        return grp, ((other // CORES) * ZS + z) * CORES + other % CORES

    def z_peer(off):
        return grp, (x * ZS + (z + off) % ZS) * CORES + core

    barrier = pltpu.get_barrier_semaphore()
    for peer in (grp_peer, red_peer, z_peer):
        for off in range(1, 8):
            pl.semaphore_signal(barrier, inc=1, device_id=peer(off), device_id_type=MESH)

    def load(c, h):
        rows = pl.ds(h * HOP, HOP)
        return pltpu.make_async_copy(snap_ref.at[c, rows], data.at[c, rows], in_sem.at[h, c])

    for h in range(NB):
        for c in range(comps):
            load(c, h).start()

    make_tables(bins_ref, tab_hi, tab_lo)

    def convert(c, h):
        load(c, h).wait()
        rows = pl.ds(h * HOP, HOP)
        high, low = split(data[c, rows])
        d_hi[c, rows] = high
        d_lo[c, rows] = low

    def transform(c, h_first, cols):
        rows = pl.ds(h_first * HOP, cols.stop - cols.start)
        high = d_hi[c, rows]
        t_hi = tab_hi[:, cols]
        return fdot(t_hi, high) + (fdot(tab_lo[:, cols], high) + fdot(t_hi, d_lo[c, rows]))

    def halo_copy(c):
        return pltpu.make_async_remote_copy(
            hsend.at[c], hrecv.at[c], h_ssem.at[c], h_rsem.at[c],
            device_id=grp_peer(GRP - 1), device_id_type=MESH,
        )

    tiles = points // 128
    comp_rows = tiles * 2 * FPG
    blk_rows = comps * comp_rows

    def rows_at(block, c, count):
        start = pl.multiple_of(block * blk_rows + c * comp_rows, 2 * FPG)
        return pl.ds(start, count * comp_rows)

    def block_copy(off, h):
        to = (grp + off) % GRP
        return pltpu.make_async_remote_copy(
            send.at[rows_at(to * NB + h, 0, comps)],
            recv.at[rows_at(grp * NB + h, 0, comps)],
            a_ssem.at[h, off], a_rsem.at[h, off],
            device_id=grp_peer(off), device_id_type=MESH,
        )

    def last_copy(off, c):
        to = (grp + off) % GRP
        return pltpu.make_async_remote_copy(
            send.at[rows_at(to * NB + NB - 1, c, 1)],
            recv.at[rows_at(grp * NB + NB - 1, c, 1)],
            a_ssem.at[NB - 1 + c, off], a_rsem.at[NB - 1 + c, off],
            device_id=grp_peer(off), device_id_type=MESH,
        )

    def own_copy(h):
        rows = rows_at(grp * NB + h, 0, comps)
        return pltpu.make_async_copy(send.at[rows], recv.at[rows], own_sem.at[h])

    def own_last(c):
        rows = rows_at(grp * NB + NB - 1, c, 1)
        return pltpu.make_async_copy(send.at[rows], recv.at[rows], own_sem.at[NB - 1 + c])

    def put(c, h, out):
        for to in range(GRP):
            for tile in range(tiles):
                rows = pl.ds((to * NB + h) * blk_rows + c * comp_rows + tile * 2 * FPG, 2 * FPG)
                send[rows, :] = out[to * 2 * FPG : (to + 1) * 2 * FPG, tile * 128 : (tile + 1) * 128]

    order = (4, 3, 5, 2, 6, 1, 7)
    both = slice(0, 2 * HOP)

    for c in range(comps):
        convert(c, 0)
        hsend[c] = transform(c, 0, slice(HOP, 2 * HOP))
        if c == 0:
            pl.semaphore_wait(barrier, 21)
        halo_copy(c).start()

    for h in range(NB - 1):
        for c in range(comps):
            convert(c, h + 1)
            put(c, h, transform(c, h, both))
        for off in order:
            block_copy(off, h).start()
        own_copy(h).start()

    for c in range(comps):
        out = transform(c, NB - 1, slice(0, HOP))
        halo_copy(c).wait_recv()
        put(c, NB - 1, out + hrecv[c])
        for off in order:
            last_copy(off, c).start()
        own_last(c).start()

    scale = jnp.sqrt(wts_ref[...] * norm)
    for h in range(NB - 1):
        own_copy(h).wait()
        for off in order:
            block_copy(off, h).wait_recv()

    def gather(c, row):
        starts = [c * comp_rows + tile * 2 * FPG + row for tile in range(tiles)]
        return jnp.concatenate(
            [recv[pl.ds(start, NBLK, stride=blk_rows), :] for start in starts], axis=1
        )

    for c in range(comps):
        own_last(c).wait()
        for off in order:
            last_copy(off, c).wait_recv()
        for f in range(FPG):
            re = gather(c, f)
            im = gather(c, FPG + f)
            both_parts = jnp.concatenate([re, im], axis=0) * scale
            high, low = split(both_parts)
            stack = jnp.concatenate([high, low], axis=0)
            prod = lax.dot_general(
                stack, stack, (((1,), (1,)), ((), ())), preferred_element_type=jnp.float32
            )
            half = prod[: 2 * NBLK] + prod[2 * NBLK :]
            gram[f] = half if c == 0 else gram[f] + half

    lane16 = lax.broadcasted_iota(jnp.int32, (NBLK // 2, 128), 1)
    lane32 = lax.broadcasted_iota(jnp.int32, (NBLK, 128), 1)
    for f in range(FPG):
        whole = gram[f]
        whole = whole + pltpu.roll(whole, 64, 1)
        low_rows = pltpu.roll(whole[NBLK:], 32, 1)
        joined = whole[:NBLK] + jnp.where((lane32 & 32) == 0, low_rows, -low_rows)
        gsend[f] = jnp.where(lane16 < 64, joined[: NBLK // 2], joined[NBLK // 2 :])

    def red_copy(off):
        return pltpu.make_async_remote_copy(
            gsend.at[(red + off) % RED], rrecv.at[red], r_ssem.at[off], r_rsem.at[off],
            device_id=red_peer(off), device_id_type=MESH,
        )

    for off in range(1, RED):
        red_copy(off).start()
    part = gsend[red]
    for off in range(1, RED):
        red_copy(off).wait_recv()
        part = part + rrecv[(red + RED - off) % RED]
    zpart[...] = part

    def z_copy(off):
        return pltpu.make_async_remote_copy(
            zpart, zrecv.at[z], z_ssem.at[off], z_rsem.at[off],
            device_id=z_peer(off), device_id_type=MESH,
        )

    for off in range(1, ZS):
        z_copy(off).start()
    zrecv[z] = part
    for off in range(1, ZS):
        z_copy(off).wait_recv()
    total = zrecv[0]
    for i in range(1, ZS):
        total = total + zrecv[i]

    rows_g = jnp.concatenate([total, pltpu.roll(total, 64, 1)], axis=0)
    upper = jnp.where(lane32 < 32, rows_g, jnp.where(lane32 < 64, -rows_g, 0.0))
    lower = jnp.where(
        lane32 < 32,
        pltpu.roll(rows_g, 96, 1),
        jnp.where(lane32 < 64, pltpu.roll(rows_g, 32, 1), 0.0),
    )
    embed = jnp.concatenate([upper, lower], axis=0)
    w = embed
    for step in range(ITERS):
        basis, lengths = orthonormalize(w)
        if step < ITERS - 1:
            padded = jnp.concatenate([basis, jnp.zeros_like(basis)], axis=0)
            w = jnp.dot(
                embed, padded, precision=lax.Precision.HIGHEST, preferred_element_type=jnp.float32
            )
    scaled = basis * (1.0 / jnp.sqrt(NBLK * lengths))
    column = jnp.concatenate([scaled, jnp.broadcast_to(lengths, scaled.shape)], axis=0)
    vsend[...] = jnp.transpose(column)[:8]

    def v_copy(off):
        return pltpu.make_async_remote_copy(
            vsend, vrecv.at[red], v_ssem.at[off], v_rsem.at[off],
            device_id=red_peer(off), device_id_type=MESH,
        )

    for off in range(1, RED):
        v_copy(off).start()
    vrecv[red] = vsend[...]
    for off in range(1, RED):
        v_copy(off).wait_recv()

    lane8 = lax.broadcasted_iota(jnp.int32, (FPG, 128), 1)
    energies = jnp.zeros((FPG, 128), jnp.float32)
    for m in range(MODES):
        cols = vrecv[:, m, :]
        for b in range(2 * NBLK):
            coef[b, m] = jnp.broadcast_to(cols[:, b : b + 1], (FPG, 128))
        energies = jnp.where(
            lane8 == m, jnp.broadcast_to(cols[:, 2 * NBLK : 2 * NBLK + 1], (FPG, 128)), energies
        )
    en_ref[...] = energies[:, :MODES]

    def mode_tile(i, carry):
        c = i // tiles
        lanes = pl.ds(pl.multiple_of((i % tiles) * 128, 128), 128)
        acc_re = [jnp.zeros((FPG, 128), jnp.float32)] * MODES
        acc_im = [jnp.zeros((FPG, 128), jnp.float32)] * MODES
        for b in range(NBLK):
            start = pl.multiple_of(b * blk_rows + i * 2 * FPG, 2 * FPG)
            x_re = recv[pl.ds(start, FPG), :]
            x_im = recv[pl.ds(start + FPG, FPG), :]
            for m in range(MODES):
                v_re = coef[b, m]
                v_im = coef[NBLK + b, m]
                acc_re[m] = acc_re[m] + (x_re * v_re - x_im * v_im)
                acc_im[m] = acc_im[m] + (x_re * v_im + x_im * v_re)
        for m in range(MODES):
            modes_ref[0, m, c, :, lanes] = acc_re[m]
            modes_ref[1, m, c, :, lanes] = acc_im[m]
        return carry

    lax.fori_loop(0, comps * tiles, mode_tile, 0)

    for c in range(comps):
        halo_copy(c).wait_send()
    for off in order:
        for h in range(NB - 1):
            block_copy(off, h).wait_send()
        for c in range(comps):
            last_copy(off, c).wait_send()
    for off in range(1, 8):
        red_copy(off).wait_send()
        z_copy(off).wait_send()
        v_copy(off).wait_send()


def shards(snapshots, kept_bins, weights):
    comps, times, points = snapshots.shape
    norm = 1.0 / (comps * points * lax.axis_size("sp"))
    f32, bf16 = jnp.float32, jnp.bfloat16
    dma = pltpu.SemaphoreType.DMA
    modes, energies = pl.pallas_call(
        functools.partial(kernel, norm),
        out_shape=(
            jax.ShapeDtypeStruct((2, MODES, comps, FPG, points), f32),
            jax.ShapeDtypeStruct((FPG, MODES), f32),
        ),
        in_specs=[
            pl.BlockSpec(memory_space=pltpu.SMEM),
            pl.BlockSpec(memory_space=pltpu.VMEM),
            pl.BlockSpec(memory_space=pl.ANY),
        ],
        out_specs=(
            pl.BlockSpec(memory_space=pltpu.VMEM),
            pl.BlockSpec(memory_space=pltpu.VMEM),
        ),
        scratch_shapes=[
            pltpu.VMEM((comps, times, points), f32),
            pltpu.VMEM((comps, times, points), bf16),
            pltpu.VMEM((comps, times, points), bf16),
            pltpu.VMEM((2 * FPG * GRP, L), bf16),
            pltpu.VMEM((2 * FPG * GRP, L), bf16),
            pltpu.VMEM((NBLK * 2 * FPG * comps * points // 128, 128), f32),
            pltpu.VMEM((NBLK * 2 * FPG * comps * points // 128, 128), f32),
            pltpu.VMEM((comps, 2 * FPG * GRP, points), f32),
            pltpu.VMEM((comps, 2 * FPG * GRP, points), f32),
            pltpu.VMEM((FPG, 2 * NBLK, 128), f32),
            pltpu.VMEM((FPG, NBLK // 2, 128), f32),
            pltpu.VMEM((RED, NBLK // 2, 128), f32),
            pltpu.VMEM((NBLK // 2, 128), f32),
            pltpu.VMEM((ZS, NBLK // 2, 128), f32),
            pltpu.VMEM((8, 128), f32),
            pltpu.VMEM((RED, 8, 128), f32),
            pltpu.VMEM((2 * NBLK, MODES, FPG, 128), f32),
            dma((NB, comps)),
            dma((NB - 1 + comps,)),
            dma((comps,)),
            dma((comps,)),
            dma((NB - 1 + comps, GRP)),
            dma((NB - 1 + comps, GRP)),
            dma((RED,)),
            dma((RED,)),
            dma((ZS,)),
            dma((ZS,)),
            dma((RED,)),
            dma((RED,)),
        ],
        compiler_params=pltpu.CompilerParams(
            collective_id=0, has_side_effects=True, vmem_limit_bytes=48 << 20
        ),
    )(kept_bins, weights.reshape(1, points), snapshots)
    return (jnp.transpose(modes, (0, 3, 1, 2, 4)), energies)


def solution(mesh):
    in_specs = (P(None, "grp", "sp"), P(), P("sp"))
    out_specs = (P(None, "grp", None, None, "sp"), P("grp", None))
    return jax.shard_map(shards, mesh=mesh, in_specs=in_specs, out_specs=out_specs, check_vma=False)
```

time: 628 us -> 106 us (0.17)
  the two profiles are of different devices: /device:TPU:2 before, /device:TPU:1 now
where the time goes in v1:
time: 106 us
  Pallas kernels  100 us (94%)
  local copies, waits for them, and re-layouts  5.12 us (5%)
    pallas_call x1, Pallas kernels, shards(): pl.pallas_call(functools.partial(kernel, norm), out_shape=(jax.ShapeDtype...  100 us
    unnamed x6, local copies, waits for them, and re-layouts  4.43 us

profile of v1, /device:TPU:1, one launch (start us, length us, event | category | flops | bytes accessed | tf_op | source)
XLA Modules:
  0.0 106.1 jit_solution(17391363879030171020)
XLA Ops:
  0.6 0.7 reshape.7.wts_ref
  1.3 0.0 copy-start
  1.3 2.3 %copy-done = f32[3,1024,384]{2,1,0:T(8,128)S(1)} copy-done((f32[3,1024,384]{2,1,0:T(8,128)S(1)}, f32[3,1024,384]{2,1,0:T(8,128)}, u32[]{:S(2)}) %copy-start) | copy-done | bytes 4718616
  3.7 0.0 copy-start.1
  3.7 0.7 copy-done.1
  4.3 100.3 %shard_map.50 = (f32[2,4,3,8,384]{4,3,2,1,0:T(8,128)S(1)}, f32[8,4]{1,0:T(8,128)S(1)}) custom-call(s32[64]{0:T(128)S(1)} %copy-done.1, f32[1,384]{1,0:T(1,128)S(1)} %reshape.7.wts_ref, f32[3,1024,384]{2,1,0:T(8,128)S(1)} %copy-done), custom_call_target="tpu_custom_call" | custom-call | tf_op jit(solution)/shard_map/pallas_call | solution.py:399
  104.6 0.8 copy.5
  105.4 0.7 copy.6
Async XLA Ops:
  1.3 2.3 %copy-start = (f32[3,1024,384]{2,1,0:T(8,128)S(1)}, f32[3,1024,384]{2,1,0:T(8,128)}, u32[]{:S(2)}) copy-start(f32[3,1024,384]{2,1,0:T(8,128)} %snap_ref.1) | copy-start | bytes 14155780
  3.7 0.7 copy-start.1

commit v2 on v1

v2 whole, which is shorter than its diff:
```python
import functools
import math

import jax
import jax.numpy as jnp
from jax import lax
from jax.experimental import pallas as pl
from jax.experimental.pallas import tpu as pltpu
from jax.sharding import PartitionSpec as P

L = 512
HOP = 256
MODES = 4
ITERS = 3
GRP = 8
FPG = 8
RED = 8
ZS = 8
CORES = 2
NB = 4
NBLK = GRP * NB
MESH = pl.DeviceIdType.MESH


def cos_sin(phase):
    quarter = (phase + 64) >> 7
    rest = (phase - (quarter << 7)).astype(jnp.float32) * (2.0 * math.pi / L)
    sq = rest * rest
    sin = rest * (1.0 + sq * (-1.0 / 6 + sq * (1.0 / 120 + sq * (-1.0 / 5040 + sq * (1.0 / 362880)))))
    cos = 1.0 + sq * (-0.5 + sq * (1.0 / 24 + sq * (-1.0 / 720 + sq * (1.0 / 40320 - sq * (1.0 / 3628800)))))
    quarter = quarter & 3
    odd = (quarter & 1) == 1
    cos_q = jnp.where(odd, sin, cos)
    sin_q = jnp.where(odd, cos, sin)
    cos_q = jnp.where((quarter == 1) | (quarter == 2), -cos_q, cos_q)
    sin_q = jnp.where(quarter >= 2, -sin_q, sin_q)
    return cos_q, sin_q


def split(x):
    high = x.astype(jnp.bfloat16)
    low = (x - high.astype(jnp.float32)).astype(jnp.bfloat16)
    return high, low


def fdot(a, b):
    return jnp.dot(a, b, preferred_element_type=jnp.float32)


def make_tables(first_group, bins_ref, tab_hi, tab_lo):
    shape = (FPG, HOP)
    row = lax.broadcasted_iota(jnp.int32, shape, 0)
    time = lax.broadcasted_iota(jnp.int32, shape, 1)
    scale = 1.0 / math.sqrt(3.0 * L / 8.0)
    window = (0.5 - 0.5 * cos_sin(time)[0]) * scale
    second = scale - window
    for off in range(GRP):
        group = (first_group + off) % GRP
        bins = jnp.full(shape, bins_ref[group * FPG], jnp.int32)
        for f in range(1, FPG):
            bins = jnp.where(row == f, bins_ref[group * FPG + f], bins)
        cos, sin = cos_sin((bins * time) & (L - 1))
        signed = jnp.where((bins & 1) == 1, -second, second)
        for half, win in ((0, window), (1, signed)):
            high, low = split(jnp.concatenate([cos * win, -sin * win], axis=0))
            rows = pl.ds(off * 2 * FPG, 2 * FPG)
            tab_hi[rows, half * HOP : (half + 1) * HOP] = high
            tab_lo[rows, half * HOP : (half + 1) * HOP] = low


def orthonormalize(w):
    lane = lax.broadcasted_iota(jnp.int32, w.shape, 1)
    lane_row = lax.broadcasted_iota(jnp.int32, (1, w.shape[1]), 1)
    w_re, w_im = w[:NBLK], w[NBLK:]
    left = w
    basis = jnp.zeros_like(w)
    lengths = jnp.ones((1, w.shape[1]), jnp.float32)
    for m in range(MODES):
        length = jnp.sqrt(jnp.sum(left * left, axis=0, keepdims=True) + 1e-06)
        unit = left / length
        basis = jnp.where(lane == m, unit, basis)
        lengths = jnp.where(lane_row == m, length, lengths)
        if m < MODES - 1:
            q = jnp.broadcast_to(unit[:, m : m + 1], w.shape)
            q_re, q_im = q[:NBLK], q[NBLK:]
            coef_re = jnp.sum(q_re * w_re + q_im * w_im, axis=0, keepdims=True)
            coef_im = jnp.sum(q_re * w_im - q_im * w_re, axis=0, keepdims=True)
            left = left - jnp.concatenate(
                [coef_re * q_re - coef_im * q_im, coef_re * q_im + coef_im * q_re], axis=0
            )
    return basis, lengths


def kernel(
    norm,
    bins_hbm,
    wts_hbm,
    snap_ref,
    modes_ref,
    en_ref,
    bins_ref,
    wts_ref,
    data,
    d_hi,
    d_lo,
    tab_hi,
    tab_lo,
    send,
    recv,
    a_send,
    d_send,
    a_keep,
    d_keep,
    a_recv,
    d_recv,
    gram,
    zs,
    gsend,
    rrecv,
    zpart,
    zrecv,
    vsend,
    vrecv,
    in_sem,
    arg_sem,
    own_sem,
    h_ssem,
    h_rsem,
    a_ssem,
    a_rsem,
    r_ssem,
    r_rsem,
    z_ssem,
    z_rsem,
    v_ssem,
    v_rsem,
):
    comps = data.shape[0]
    points = data.shape[2]
    tiles = points // 128
    comp_rows = tiles * 2 * FPG
    blk_rows = comps * comp_rows
    half_rows = GRP * FPG
    grp = lax.axis_index("grp")
    sp = lax.axis_index("sp")
    core = sp % CORES
    z = (sp // CORES) % ZS
    x = sp // (CORES * ZS)
    red = x * CORES + core

    def grp_peer(off):
        return (grp + off) % GRP, sp

    def red_peer(off):
        other = (red + off) % RED
        return grp, ((other // CORES) * ZS + z) * CORES + other % CORES

    def z_peer(off):
        return grp, (x * ZS + (z + off) % ZS) * CORES + core

    bins_copy = pltpu.make_async_copy(bins_hbm, bins_ref, arg_sem.at[0])
    wts_copy = pltpu.make_async_copy(wts_hbm, wts_ref, arg_sem.at[1])
    bins_copy.start()

    def load(c, h):
        rows = pl.ds(h * HOP, HOP)
        return pltpu.make_async_copy(snap_ref.at[c, rows], data.at[c, rows], in_sem.at[h, c])

    for h in (0, NB - 1):
        for c in range(comps):
            load(c, h).start()
    barrier = pltpu.get_barrier_semaphore()
    for off in (4, 3, 5, 2, 6, 1, 7):
        for peer in (grp_peer, z_peer, red_peer):
            pl.semaphore_signal(barrier, inc=1, device_id=peer(off), device_id_type=MESH)
    for h in range(1, NB - 1):
        for c in range(comps):
            load(c, h).start()
    wts_copy.start()

    bins_copy.wait()
    make_tables(grp, bins_ref, tab_hi, tab_lo)

    def convert(c, h):
        load(c, h).wait()
        rows = pl.ds(h * HOP, HOP)
        high, low = split(data[c, rows])
        d_hi[c, rows] = high
        d_lo[c, rows] = low

    def transform(c, h_first, cols):
        rows = pl.ds(h_first * HOP, cols.stop - cols.start)
        high = d_hi[c, rows]
        t_hi = tab_hi[:, cols]
        return fdot(t_hi, high) + (fdot(tab_lo[:, cols], high) + fdot(t_hi, d_lo[c, rows]))

    def a_copy(c):
        return pltpu.make_async_remote_copy(
            a_send.at[c], a_recv.at[c], h_ssem.at[0, c], h_rsem.at[0, c],
            device_id=grp_peer(1), device_id_type=MESH,
        )

    def d_copy(c):
        return pltpu.make_async_remote_copy(
            d_send.at[c], d_recv.at[c], h_ssem.at[1, c], h_rsem.at[1, c],
            device_id=grp_peer(GRP - 1), device_id_type=MESH,
        )

    def rows_at(block, c, count):
        start = pl.multiple_of(block * blk_rows + c * comp_rows, 2 * FPG)
        return pl.ds(start, count * comp_rows)

    def block_copy(off, h):
        return pltpu.make_async_remote_copy(
            send.at[rows_at(off * NB + h, 0, comps)],
            recv.at[rows_at(grp * NB + h, 0, comps)],
            a_ssem.at[h, off], a_rsem.at[h, off],
            device_id=grp_peer(off), device_id_type=MESH,
        )

    left_block = (grp * NB + NBLK - 1) % NBLK
    right_block = grp * NB + NB - 1

    def edge_copy(off, c):
        return pltpu.make_async_remote_copy(
            send.at[rows_at(off * NB + NB - 1, c, 1)],
            recv.at[rows_at(left_block if off < 4 else right_block, c, 1)],
            a_ssem.at[NB - 1 + c, off], a_rsem.at[NB - 1 + c, off],
            device_id=grp_peer(off), device_id_type=MESH,
        )

    def own_copy(h):
        return pltpu.make_async_copy(
            send.at[rows_at(h, 0, comps)], recv.at[rows_at(grp * NB + h, 0, comps)], own_sem.at[h]
        )

    def own_edge(c, side):
        return pltpu.make_async_copy(
            send.at[rows_at(side * 4 * NB + NB - 1, c, 1)],
            recv.at[rows_at(right_block if side else left_block, c, 1)],
            own_sem.at[NB - 1 + c * 2 + side],
        )

    def put(c, h, off, rows):
        for tile in range(tiles):
            at = pl.ds((off * NB + h) * blk_rows + c * comp_rows + tile * 2 * FPG, 2 * FPG)
            send[at, :] = rows[:, tile * 128 : (tile + 1) * 128]

    order = (4, 3, 5, 2, 6, 1, 7)
    edges = (3, 5, 2, 6, 1, 7)
    both = slice(0, 2 * HOP)
    unit = 2 * FPG

    for c in range(comps):
        convert(c, 0)
        out = transform(c, 0, slice(HOP, 2 * HOP))
        d_keep[c] = out[:half_rows]
        d_send[c] = out[half_rows:]
        convert(c, NB - 1)
        out = transform(c, NB - 1, slice(0, HOP))
        a_send[c] = out[unit : unit + half_rows]
        a_keep[c, :unit] = out[:unit]
        a_keep[c, unit:] = out[unit + half_rows :]

    for h in range(NB - 1):
        for c in range(comps):
            if h + 1 < NB - 1:
                convert(c, h + 1)
            out = transform(c, h, both)
            for off in range(GRP):
                put(c, h, off, out[off * unit : (off + 1) * unit])
        if h == 0:
            pl.semaphore_wait(barrier, 21)
            for c in range(comps):
                a_copy(c).start()
                d_copy(c).start()
        for off in order:
            block_copy(off, h).start()
        own_copy(h).start()

    for c in range(comps):
        a_copy(c).wait_recv()
        for off in range(4):
            put(c, NB - 1, off, d_keep[c, off * unit : (off + 1) * unit] + a_recv[c, off * unit : (off + 1) * unit])
        d_copy(c).wait_recv()
        for off, slot in ((4, 0), (5, 1), (6, 2), (7, 3)):
            mine = a_keep[c, slot * unit : (slot + 1) * unit]
            at = 3 if off == 4 else off - 5
            put(c, NB - 1, off, mine + d_recv[c, at * unit : (at + 1) * unit])
        for off in edges:
            edge_copy(off, c).start()
        own_edge(c, 0).start()
        own_edge(c, 1).start()

    wts_copy.wait()
    scale = jnp.sqrt(wts_ref[...].reshape(1, points) * norm)
    for h in range(NB - 1):
        own_copy(h).wait()
        for off in order:
            block_copy(off, h).wait_recv()

    def gather(c, row):
        starts = [c * comp_rows + tile * 2 * FPG + row for tile in range(tiles)]
        return jnp.concatenate(
            [recv[pl.ds(start, NBLK, stride=blk_rows), :] for start in starts], axis=1
        )

    def red_copy(off):
        return pltpu.make_async_remote_copy(
            gsend.at[(red + off) % RED], rrecv.at[red], r_ssem.at[off], r_rsem.at[off],
            device_id=red_peer(off), device_id_type=MESH,
        )

    lane16 = lax.broadcasted_iota(jnp.int32, (NBLK // 2, 128), 1)
    lane32 = lax.broadcasted_iota(jnp.int32, (NBLK, 128), 1)
    for c in range(comps):
        own_edge(c, 0).wait()
        own_edge(c, 1).wait()
        for off in edges:
            edge_copy(off, c).wait_recv()
        for f in range(FPG):
            high, low = split(jnp.concatenate([gather(c, f), gather(c, FPG + f)], axis=0) * scale)
            stack = jnp.concatenate([high, low], axis=0)
            zs[f, c] = stack
            prod = lax.dot_general(
                stack, stack, (((1,), (1,)), ((), ())), preferred_element_type=jnp.float32
            )
            whole = prod[: 2 * NBLK] + prod[2 * NBLK :]
            if c > 0:
                whole = gram[f] + whole
            if c < comps - 1:
                gram[f] = whole
                continue
            whole = whole + pltpu.roll(whole, 64, 1)
            low_rows = pltpu.roll(whole[NBLK:], 32, 1)
            joined = whole[:NBLK] + jnp.where((lane32 & 32) == 0, low_rows, -low_rows)
            gsend[f] = jnp.where(lane16 < 64, joined[: NBLK // 2], joined[NBLK // 2 :])

            @pl.when(red != f)
            def _():
                red_copy((f + RED - red) % RED).start()

    part = gsend[red]
    for off in range(1, RED):
        red_copy(off).wait_recv()
        part = part + rrecv[(red + RED - off) % RED]
    zpart[...] = part

    def z_copy(off):
        return pltpu.make_async_remote_copy(
            zpart, zrecv.at[z], z_ssem.at[off], z_rsem.at[off],
            device_id=z_peer(off), device_id_type=MESH,
        )

    for off in (4, 3, 5, 2, 6, 1, 7):
        z_copy(off).start()
    zrecv[z] = part
    for off in range(1, ZS):
        z_copy(off).wait_recv()
    total = zrecv[0]
    for i in range(1, ZS):
        total = total + zrecv[i]

    rows_g = jnp.concatenate([total, pltpu.roll(total, 64, 1)], axis=0)
    upper = jnp.where(lane32 < 32, rows_g, jnp.where(lane32 < 64, -rows_g, 0.0))
    lower = jnp.where(
        lane32 < 32,
        pltpu.roll(rows_g, 96, 1),
        jnp.where(lane32 < 64, pltpu.roll(rows_g, 32, 1), 0.0),
    )
    embed = jnp.concatenate([upper, lower], axis=0)
    w = embed
    for step in range(ITERS):
        basis, lengths = orthonormalize(w)
        if step < ITERS - 1:
            padded = jnp.concatenate([basis, jnp.zeros_like(basis)], axis=0)
            w = jnp.dot(
                embed, padded, precision=lax.Precision.HIGHEST, preferred_element_type=jnp.float32
            )
    scaled = basis * (1.0 / jnp.sqrt(NBLK * lengths))
    v_re, v_im = scaled[:NBLK], scaled[NBLK:]
    swapped = pltpu.roll(jnp.concatenate([v_im, v_re], axis=0), MODES, 1)
    lane64 = lax.broadcasted_iota(jnp.int32, scaled.shape, 1)
    factors = jnp.where(lane64 < MODES, jnp.concatenate([v_re, -v_im], axis=0), swapped)
    column = jnp.concatenate([factors, jnp.broadcast_to(lengths, scaled.shape)], axis=0)
    vsend[...] = jnp.transpose(column)[: 2 * MODES]

    def v_copy(off):
        return pltpu.make_async_remote_copy(
            vsend, vrecv.at[red], v_ssem.at[off], v_rsem.at[off],
            device_id=red_peer(off), device_id_type=MESH,
        )

    for off in range(1, RED):
        v_copy(off).start()
    vrecv[red] = vsend[...]
    for off in range(1, RED):
        v_copy(off).wait_recv()

    lane8 = lax.broadcasted_iota(jnp.int32, (2 * MODES, 128), 1)
    unscale = 1.0 / scale
    energies = jnp.zeros((2 * MODES, 128), jnp.float32)
    for f in range(FPG):
        v = vrecv[f]
        energies = jnp.where(
            lane8 == f, jnp.broadcast_to(v[:, 2 * NBLK : 2 * NBLK + 1], v.shape), energies
        )
        v_hi = v.astype(jnp.bfloat16).astype(jnp.float32)
        first = jnp.where(lane8 < 64, v_hi, pltpu.roll(v_hi, 64, 1))
        rest = jnp.where(lane8 < 64, v - v_hi, 0.0)
        factor = jnp.concatenate([first, rest], axis=0).astype(jnp.bfloat16)
        for c in range(comps):
            out = fdot(factor, zs[f, c])
            out = (out[: 2 * MODES] + out[2 * MODES :]) * unscale
            modes_ref[0, f, c] = out[:MODES]
            modes_ref[1, f, c] = out[MODES:]
    en_ref[...] = energies[:MODES, :FPG]

    for c in range(comps):
        a_copy(c).wait_send()
        d_copy(c).wait_send()
        for off in edges:
            edge_copy(off, c).wait_send()
    for off in order:
        for h in range(NB - 1):
            block_copy(off, h).wait_send()
        red_copy(off).wait_send()
        z_copy(off).wait_send()
        v_copy(off).wait_send()


def shards(snapshots, kept_bins, weights):
    comps, times, points = snapshots.shape
    norm = 1.0 / (comps * points * lax.axis_size("sp"))
    f32, bf16 = jnp.float32, jnp.bfloat16
    dma = pltpu.SemaphoreType.DMA
    half = pltpu.VMEM((comps, GRP * FPG, points), f32)
    spectra = pltpu.VMEM((NBLK * 2 * FPG * comps * points // 128, 128), f32)
    table = pltpu.VMEM((2 * FPG * GRP, L), bf16)
    small = pltpu.VMEM((RED, NBLK // 2, 128), f32)
    n_msg = NB - 1 + comps
    hbm = pl.BlockSpec(memory_space=pltpu.HBM)
    vmem = pl.BlockSpec(memory_space=pltpu.VMEM)
    modes, energies = pl.pallas_call(
        functools.partial(kernel, norm),
        out_shape=(
            jax.ShapeDtypeStruct((2, FPG, comps, MODES, points), f32),
            jax.ShapeDtypeStruct((MODES, FPG), f32),
        ),
        in_specs=[hbm, hbm, hbm],
        out_specs=(vmem, vmem),
        scratch_shapes=[
            pltpu.SMEM((GRP * FPG,), jnp.int32),
            pltpu.VMEM((points,), f32),
            pltpu.VMEM((comps, times, points), f32),
            pltpu.VMEM((comps, times, points), bf16),
            pltpu.VMEM((comps, times, points), bf16),
            table,
            table,
            spectra,
            spectra,
            half,
            half,
            half,
            half,
            half,
            half,
            pltpu.VMEM((FPG, 2 * NBLK, 128), f32),
            pltpu.VMEM((FPG, comps, 4 * NBLK, points), bf16),
            small,
            small,
            pltpu.VMEM((NBLK // 2, 128), f32),
            small,
            pltpu.VMEM((8, 128), f32),
            pltpu.VMEM((RED, 8, 128), f32),
            dma((NB, comps)),
            dma((2,)),
            dma((NB - 1 + 2 * comps,)),
            dma((2, comps)),
            dma((2, comps)),
            dma((n_msg, GRP)),
            dma((n_msg, GRP)),
            dma((RED,)),
            dma((RED,)),
            dma((ZS,)),
            dma((ZS,)),
            dma((RED,)),
            dma((RED,)),
        ],
        compiler_params=pltpu.CompilerParams(
            collective_id=0, has_side_effects=True, vmem_limit_bytes=48 << 20
        ),
    )(*[pltpu.with_memory_space_constraint(a, pltpu.HBM) for a in (kept_bins, weights, snapshots)])
    return (jnp.transpose(modes, (0, 1, 3, 2, 4)), jnp.transpose(energies))


def solution(mesh):
    in_specs = (P(None, "grp", "sp"), P(), P("sp"))
    out_specs = (P(None, "grp", None, None, "sp"), P("grp", None))
    return jax.shard_map(shards, mesh=mesh, in_specs=in_specs, out_specs=out_specs, check_vma=False)
```

time: 106 us -> 91.4 us (0.86)
  Pallas kernels: 100 us -> 89.4 us
  local copies, waits for them, and re-layouts: 5.12 us -> 1.29 us
    pallas_call x1, Pallas kernels: 100 us -> 89.4 us  [shards(): pl.pallas_call(functools.partial(kernel, norm), out_shape=(jax.ShapeDtype...]
    unnamed x6 -> x2, local copies, waits for them, and re-layouts: 4.43 us -> 1.29 us
where the time goes in v2:
time: 91.4 us; the launch traced here: 91.3 us
  Pallas kernels  89.4 us (98%)
  local copies, waits for them, and re-layouts  1.29 us (1%)
    pallas_call x1, Pallas kernels, shards(): pl.pallas_call(functools.partial(kernel, norm), out_shape=(jax.ShapeDtype...  89.4 us

profile of v2, /device:TPU:1, one launch (start us, length us, event | category | flops | bytes accessed | tf_op | source)
XLA Modules:
  0.0 91.3 jit_solution(4589059949838342569)
XLA Ops:
  0.6 89.4 %shard_map.50 = (f32[2,8,3,4,384]{4,3,2,1,0:T(4,128)S(1)}, f32[4,8]{1,0:T(4,128)S(1)}) custom-call(s32[64]{0:T(128)} %bins_hbm.1, f32[384]{0:T(512)} %wts_hbm.1, f32[3,1024,384]{2,1,0:T(8,128)} %snap_ref.1), custom_call_target="tpu_custom_call" | custom-call | tf_op jit(solution)/shard_map/pallas_call | solution.py:444
  90.0 0.7 copy.7
  90.7 0.6 copy.8

commit v3 on v2

v3 whole, which is shorter than its diff:
```python
import functools
import math

import jax
import jax.numpy as jnp
from jax import lax
from jax.experimental import pallas as pl
from jax.experimental.pallas import tpu as pltpu
from jax.sharding import PartitionSpec as P

L = 512
HOP = 256
MODES = 4
ITERS = 3
GRP = 8
FPG = 8
STAGES = 2
FPS = 4
RED = 8
ZS = 8
CORES = 2
NB = 4
NBLK = GRP * NB
MESH = pl.DeviceIdType.MESH


def cos_sin(phase):
    quarter = (phase + 64) >> 7
    rest = (phase - (quarter << 7)).astype(jnp.float32) * (2.0 * math.pi / L)
    sq = rest * rest
    sin = rest * (1.0 + sq * (-1.0 / 6 + sq * (1.0 / 120 + sq * (-1.0 / 5040 + sq * (1.0 / 362880)))))
    cos = 1.0 + sq * (-0.5 + sq * (1.0 / 24 + sq * (-1.0 / 720 + sq * (1.0 / 40320 - sq * (1.0 / 3628800)))))
    quarter = quarter & 3
    odd = (quarter & 1) == 1
    cos_q = jnp.where(odd, sin, cos)
    sin_q = jnp.where(odd, cos, sin)
    cos_q = jnp.where((quarter == 1) | (quarter == 2), -cos_q, cos_q)
    sin_q = jnp.where(quarter >= 2, -sin_q, sin_q)
    return cos_q, sin_q


def split(x):
    high = x.astype(jnp.bfloat16)
    low = (x - high.astype(jnp.float32)).astype(jnp.bfloat16)
    return high, low


def fdot(a, b):
    return jnp.dot(a, b, preferred_element_type=jnp.float32)


def make_tables(first_group, bins_ref, tab_hi, tab_lo):
    shape = (2 * FPS, HOP)
    row = lax.broadcasted_iota(jnp.int32, shape, 0)
    time = lax.broadcasted_iota(jnp.int32, shape, 1)
    scale = 1.0 / math.sqrt(3.0 * L / 8.0)
    window = (0.5 - 0.5 * cos_sin(time)[0]) * scale
    second = scale - window
    for off in range(GRP):
        group = (first_group + off) % GRP
        waves = [], []
        for stage in range(STAGES):
            first = group * FPG + stage * FPS
            bins = jnp.full(shape, bins_ref[first], jnp.int32)
            for f in range(1, FPS):
                bins = jnp.where((row & (FPS - 1)) == f, bins_ref[first + f], bins)
            cos, sin = cos_sin((bins * time) & (L - 1))
            wave = jnp.where(row < FPS, cos, -sin)
            waves[0].append(wave * window)
            waves[1].append(wave * jnp.where((bins & 1) == 1, -second, second))
        for half in range(2):
            high, low = split(jnp.concatenate(waves[half], axis=0))
            rows = pl.ds(off * 2 * FPG, 2 * FPG)
            tab_hi[rows, half * HOP : (half + 1) * HOP] = high
            tab_lo[rows, half * HOP : (half + 1) * HOP] = low


def orthonormalize(w):
    lane = lax.broadcasted_iota(jnp.int32, w.shape, 1)
    lane_row = lax.broadcasted_iota(jnp.int32, (1, w.shape[1]), 1)
    w_re, w_im = w[:NBLK], w[NBLK:]
    left = w
    basis = jnp.zeros_like(w)
    lengths = jnp.ones((1, w.shape[1]), jnp.float32)
    for m in range(MODES):
        length = jnp.sqrt(jnp.sum(left * left, axis=0, keepdims=True) + 1e-06)
        unit = left / length
        basis = jnp.where(lane == m, unit, basis)
        lengths = jnp.where(lane_row == m, length, lengths)
        if m < MODES - 1:
            q = jnp.broadcast_to(unit[:, m : m + 1], w.shape)
            q_re, q_im = q[:NBLK], q[NBLK:]
            coef_re = jnp.sum(q_re * w_re + q_im * w_im, axis=0, keepdims=True)
            coef_im = jnp.sum(q_re * w_im - q_im * w_re, axis=0, keepdims=True)
            left = left - jnp.concatenate(
                [coef_re * q_re - coef_im * q_im, coef_re * q_im + coef_im * q_re], axis=0
            )
    return basis, lengths


def pack(whole, lane, row):
    whole = whole + pltpu.roll(whole, 64, 1)
    low_rows = pltpu.roll(whole[NBLK:], 32, 1)
    even = (lane & 32) == 0
    joined = whole[:NBLK] + jnp.where(even, low_rows, -low_rows)
    other = pltpu.roll(joined, 32, 1)
    tri = jnp.where((row <= (lane & 31)) == even, joined, other)
    tile = tri[:8]
    lane8 = lane[:8]
    for i in range(1, 4):
        tile = jnp.where(lane8 >= 32 * i, tri[8 * i : 8 * i + 8], tile)
    return tile


def unpack(tile, lane, row):
    tri = jnp.concatenate([tile] + [pltpu.roll(tile, 128 - 32 * i, 1) for i in range(1, 4)], axis=0)
    flipped = jnp.transpose(jnp.concatenate([tri, jnp.zeros((96, 128), jnp.float32)], axis=0))[:NBLK]
    g_re = jnp.where(row <= lane, tri, flipped)
    g_im = jnp.where(row > lane, tri, jnp.where(row < lane, -flipped, 0.0))
    right_re = jnp.where(lane < 64, pltpu.roll(g_re, 32, 1), 0.0)
    right_im = jnp.where(lane < 64, pltpu.roll(g_im, 32, 1), 0.0)
    upper = jnp.where(lane < 32, g_re, -right_im)
    lower = jnp.where(lane < 32, g_im, right_re)
    return jnp.concatenate([upper, lower], axis=0)


def subspace(embed):
    w = embed
    for step in range(ITERS):
        basis, lengths = orthonormalize(w)
        if step < ITERS - 1:
            padded = jnp.concatenate([basis, jnp.zeros_like(basis)], axis=0)
            w = jnp.dot(
                embed, padded, precision=lax.Precision.HIGHEST, preferred_element_type=jnp.float32
            )
    scaled = basis * (1.0 / jnp.sqrt(NBLK * lengths))
    v_re, v_im = scaled[:NBLK], scaled[NBLK:]
    swapped = pltpu.roll(jnp.concatenate([v_im, v_re], axis=0), MODES, 1)
    lane64 = lax.broadcasted_iota(jnp.int32, scaled.shape, 1)
    factors = jnp.where(lane64 < MODES, jnp.concatenate([v_re, -v_im], axis=0), swapped)
    column = jnp.concatenate([factors, jnp.broadcast_to(lengths, scaled.shape)], axis=0)
    return jnp.transpose(column)[: 2 * MODES]


def kernel(
    norm,
    bins_hbm,
    wts_hbm,
    snap_ref,
    modes_ref,
    en_ref,
    bins_ref,
    wts_ref,
    data,
    d_hi,
    d_lo,
    tab_hi,
    tab_lo,
    send,
    recv,
    a_send,
    d_send,
    a_keep,
    d_keep,
    a_recv,
    d_recv,
    zs,
    gsend,
    rrecv,
    zpart,
    zrecv,
    vsend,
    vrecv,
    in_sem,
    arg_sem,
    own_sem,
    h_ssem,
    h_rsem,
    a_ssem,
    a_rsem,
    e_ssem,
    e_rsem,
    r_ssem,
    r_rsem,
    z_ssem,
    z_rsem,
    v_ssem,
    v_rsem,
):
    comps = data.shape[0]
    points = data.shape[2]
    tiles = points // 128
    comp_rows = tiles * 2 * FPS
    blk_rows = comps * comp_rows
    half_rows = GRP * FPG
    grp = lax.axis_index("grp")
    sp = lax.axis_index("sp")
    core = sp % CORES
    z = (sp // CORES) % ZS
    x = sp // (CORES * ZS)
    red = x * CORES + core

    def grp_peer(off):
        return (grp + off) % GRP, sp

    def red_peer(off):
        other = (red + off) % RED
        return grp, ((other // CORES) * ZS + z) * CORES + other % CORES

    def z_peer(off):
        return grp, (x * ZS + (z + off) % ZS) * CORES + core

    bins_copy = pltpu.make_async_copy(bins_hbm, bins_ref, arg_sem.at[0])
    wts_copy = pltpu.make_async_copy(wts_hbm, wts_ref, arg_sem.at[1])
    bins_copy.start()
    barrier = pltpu.get_barrier_semaphore()
    for off in (4, 3, 5, 2, 6, 1, 7):
        pl.semaphore_signal(barrier, inc=1, device_id=grp_peer(off), device_id_type=MESH)

    def load(c, h):
        rows = pl.ds(h * HOP, HOP)
        return pltpu.make_async_copy(snap_ref.at[c, rows], data.at[c, rows], in_sem.at[h, c])

    for h in (0, NB - 1):
        for c in range(comps):
            load(c, h).start()
    for off in (4, 3, 5, 2, 6, 1, 7):
        for peer in (z_peer, red_peer):
            pl.semaphore_signal(barrier, inc=1, device_id=peer(off), device_id_type=MESH)
    for h in range(1, NB - 1):
        for c in range(comps):
            load(c, h).start()
    wts_copy.start()

    bins_copy.wait()
    make_tables(grp, bins_ref, tab_hi, tab_lo)

    def convert(c, h):
        load(c, h).wait()
        rows = pl.ds(h * HOP, HOP)
        high, low = split(data[c, rows])
        d_hi[c, rows] = high
        d_lo[c, rows] = low

    def transform(c, h_first, cols):
        rows = pl.ds(h_first * HOP, cols.stop - cols.start)
        high = d_hi[c, rows]
        t_hi = tab_hi[:, cols]
        return fdot(t_hi, high) + (fdot(tab_lo[:, cols], high) + fdot(t_hi, d_lo[c, rows]))

    a_copy = pltpu.make_async_remote_copy(
        a_send, a_recv, h_ssem.at[0], h_rsem.at[0], device_id=grp_peer(1), device_id_type=MESH
    )
    d_copy = pltpu.make_async_remote_copy(
        d_send, d_recv, h_ssem.at[1], h_rsem.at[1], device_id=grp_peer(GRP - 1), device_id_type=MESH
    )
    left_block = (grp * NB + NBLK - 1) % NBLK
    right_block = grp * NB + NB - 1

    def sent(stage, off, h):
        return pl.ds(((stage * GRP + off) * NB + h) * blk_rows, blk_rows)

    def landed(stage, block):
        return pl.ds(pl.multiple_of((stage * NBLK + block) * blk_rows, 8), blk_rows)

    def target(off, h):
        if h < NB - 1:
            return grp * NB + h
        return left_block if off < 4 else right_block

    def block_copy(stage, off, h):
        return pltpu.make_async_remote_copy(
            send.at[sent(stage, off, h)], recv.at[landed(stage, target(off, h))],
            a_ssem.at[stage * NB + h, off], a_rsem.at[stage * NB + h, off],
            device_id=grp_peer(off), device_id_type=MESH,
        )

    def edge_copy(off, c):
        rows = c * comp_rows
        return pltpu.make_async_remote_copy(
            send.at[pl.ds(((GRP + off) * NB + NB - 1) * blk_rows + rows, comp_rows)],
            recv.at[
                pl.ds(
                    pl.multiple_of((NBLK + target(off, NB - 1)) * blk_rows + rows, 8), comp_rows
                )
            ],
            e_ssem.at[c, off], e_rsem.at[c, off],
            device_id=grp_peer(off), device_id_type=MESH,
        )

    def own_copy(stage, h):
        off, h_from = (4, NB - 1) if h == NB else (0, h)
        return pltpu.make_async_copy(
            send.at[sent(stage, off, h_from)], recv.at[landed(stage, target(off, h_from))],
            own_sem.at[stage, h],
        )

    def put(c, h, off, rows):
        for stage in range(STAGES):
            for tile in range(tiles):
                start = ((stage * GRP + off) * NB + h) * blk_rows + c * comp_rows + tile * 2 * FPS
                send[pl.ds(start, 2 * FPS), :] = rows[
                    stage * 2 * FPS : (stage + 1) * 2 * FPS, tile * 128 : (tile + 1) * 128
                ]

    def offsets(h):
        return edges if h == NB - 1 else order

    def start_sends(stage, h):
        if stage == STAGES - 1 and h == NB - 1:
            for c in range(comps):
                for off in edges:
                    edge_copy(off, c).start()
        else:
            for off in offsets(h):
                block_copy(stage, off, h).start()
        own_copy(stage, h).start()
        if h == NB - 1:
            own_copy(stage, NB).start()

    order = (4, 3, 5, 2, 6, 1, 7)
    edges = (3, 5, 2, 6, 1, 7)
    both = slice(0, 2 * HOP)
    unit = 2 * FPG

    for c in range(comps):
        convert(c, 0)
        out = transform(c, 0, slice(HOP, 2 * HOP))
        d_keep[c] = out[:half_rows]
        d_send[c] = out[half_rows:]
        convert(c, NB - 1)
        out = transform(c, NB - 1, slice(0, HOP))
        a_send[c] = out[unit : unit + half_rows]
        a_keep[c, :unit] = out[:unit]
        a_keep[c, unit:] = out[unit + half_rows :]
    pl.semaphore_wait(barrier, 21)
    a_copy.start()
    d_copy.start()

    for h in range(NB - 1):
        for c in range(comps):
            if h + 1 < NB - 1:
                convert(c, h + 1)
            out = transform(c, h, both)
            for off in range(GRP):
                put(c, h, off, out[off * unit : (off + 1) * unit])
        start_sends(0, h)

    a_copy.wait_recv()
    d_copy.wait_recv()
    for c in range(comps):
        for off in range(4):
            rows = slice(off * unit, (off + 1) * unit)
            put(c, NB - 1, off, d_keep[c, rows] + a_recv[c, rows])
        for off, slot in ((4, 0), (5, 1), (6, 2), (7, 3)):
            mine = a_keep[c, slot * unit : (slot + 1) * unit]
            at = 3 if off == 4 else off - 5
            put(c, NB - 1, off, mine + d_recv[c, at * unit : (at + 1) * unit])
    start_sends(0, NB - 1)
    for h in range(NB):
        start_sends(1, h)

    wts_copy.wait()
    scale = jnp.sqrt(wts_ref[...].reshape(1, points) * norm)
    unscale = 1.0 / scale
    lane32 = lax.broadcasted_iota(jnp.int32, (NBLK, 128), 1)
    row32 = lax.broadcasted_iota(jnp.int32, (NBLK, 128), 0)
    lane8 = lax.broadcasted_iota(jnp.int32, (2 * MODES, 128), 1)

    def gather(stage, c, row):
        starts = [stage * NBLK * blk_rows + c * comp_rows + tile * 2 * FPS + row for tile in range(tiles)]
        return jnp.concatenate(
            [recv[pl.ds(start, NBLK, stride=blk_rows), :] for start in starts], axis=1
        )

    def red_copy(stage, off):
        pair = pl.ds(((core + off) % CORES) * 2, 2)
        return pltpu.make_async_remote_copy(
            gsend.at[stage, pair], rrecv.at[stage, red], r_ssem.at[stage, off], r_rsem.at[stage, off],
            device_id=red_peer(off), device_id_type=MESH,
        )

    def z_copy(stage, off):
        return pltpu.make_async_remote_copy(
            zpart.at[stage], zrecv.at[stage, z], z_ssem.at[stage, off], z_rsem.at[stage, off],
            device_id=z_peer(off), device_id_type=MESH,
        )

    def v_copy(stage):
        return pltpu.make_async_remote_copy(
            vsend.at[stage], vrecv.at[stage, core], v_ssem.at[stage], v_rsem.at[stage],
            device_id=(grp, sp + 1 - 2 * core), device_id_type=MESH,
        )

    def finish_sends():
        a_copy.wait_send()
        d_copy.wait_send()
        for stage in range(STAGES):
            for h in range(NB - 1 if stage == STAGES - 1 else NB):
                for off in offsets(h):
                    block_copy(stage, off, h).wait_send()
        for c in range(comps):
            for off in edges:
                edge_copy(off, c).wait_send()

    energies = jnp.zeros((2 * MODES, 128), jnp.float32)
    for stage in range(STAGES):
        last = stage == STAGES - 1
        for h in range(NB + 1):
            own_copy(stage, h).wait()
        for h in range(NB - 1 if last else NB):
            for off in offsets(h):
                block_copy(stage, off, h).wait_recv()

        whole = [None] * FPS
        for c in range(comps):
            if last:
                for off in edges:
                    edge_copy(off, c).wait_recv()
            for f in range(FPS):
                parts = [gather(stage, c, f), gather(stage, c, FPS + f)]
                high, low = split(jnp.concatenate(parts, axis=0) * scale)
                stack = jnp.concatenate([high, low], axis=0)
                zs[stage * FPS + f, c] = stack
                prod = lax.dot_general(
                    stack, stack, (((1,), (1,)), ((), ())), preferred_element_type=jnp.float32
                )
                half = prod[: 2 * NBLK] + prod[2 * NBLK :]
                whole[f] = half if c == 0 else whole[f] + half
        for f in range(FPS):
            gsend[stage, f] = pack(whole[f], lane32, row32)

        for off in (4, 3, 5, 2, 6, 1, 7):
            red_copy(stage, off).start()
        rrecv[stage, red] = gsend[stage, pl.ds(core * 2, 2)]
        if last:
            finish_sends()
        for off in range(1, RED):
            red_copy(stage, off).wait_recv()
        part = rrecv[stage, 0]
        for i in range(1, RED):
            part = part + rrecv[stage, i]
        zpart[stage] = part
        for off in (4, 3, 5, 2, 6, 1, 7):
            z_copy(stage, off).start()
        zrecv[stage, z] = part
        for off in range(1, RED):
            red_copy(stage, off).wait_send()
        for off in range(1, ZS):
            z_copy(stage, off).wait_recv()
        total = zrecv[stage, 0]
        for i in range(1, ZS):
            total = total + zrecv[stage, i]

        factors = jnp.stack([subspace(unpack(total[j], lane32, row32)) for j in range(2)])
        vsend[stage] = factors
        v_copy(stage).start()
        vrecv[stage, core] = factors
        for off in range(1, ZS):
            z_copy(stage, off).wait_send()

        for f in range(FPS):
            if f == 2:
                v_copy(stage).wait()
            worker = core if f < 2 else 1 - core
            v = vrecv[stage, worker, f % 2]
            bin_at = stage * FPS + worker * 2 + f % 2
            energies = jnp.where(
                lane8 == bin_at, jnp.broadcast_to(v[:, 2 * NBLK : 2 * NBLK + 1], v.shape), energies
            )
            v_hi = v.astype(jnp.bfloat16).astype(jnp.float32)
            first = jnp.where(lane8 < 64, v_hi, pltpu.roll(v_hi, 64, 1))
            rest = jnp.where(lane8 < 64, v - v_hi, 0.0)
            factor = jnp.concatenate([first, rest], axis=0).astype(jnp.bfloat16)
            for c in range(comps):
                out = fdot(factor, zs[bin_at, c])
                out = (out[: 2 * MODES] + out[2 * MODES :]) * unscale
                modes_ref[0, bin_at, c] = out[:MODES]
                modes_ref[1, bin_at, c] = out[MODES:]
    en_ref[...] = energies[:MODES, :FPG]


def shards(snapshots, kept_bins, weights):
    comps, times, points = snapshots.shape
    norm = 1.0 / (comps * points * lax.axis_size("sp"))
    f32, bf16 = jnp.float32, jnp.bfloat16
    dma = pltpu.SemaphoreType.DMA
    half = pltpu.VMEM((comps, GRP * FPG, points), f32)
    spectra = pltpu.VMEM((NBLK * 2 * FPG * comps * points // 128, 128), f32)
    table = pltpu.VMEM((2 * FPG * GRP, L), bf16)
    hbm = pl.BlockSpec(memory_space=pltpu.HBM)
    vmem = pl.BlockSpec(memory_space=pltpu.VMEM)
    modes, energies = pl.pallas_call(
        functools.partial(kernel, norm),
        out_shape=(
            jax.ShapeDtypeStruct((2, FPG, comps, MODES, points), f32),
            jax.ShapeDtypeStruct((MODES, FPG), f32),
        ),
        in_specs=[hbm, hbm, hbm],
        out_specs=(vmem, vmem),
        scratch_shapes=[
            pltpu.SMEM((GRP * FPG,), jnp.int32),
            pltpu.VMEM((points,), f32),
            pltpu.VMEM((comps, times, points), f32),
            pltpu.VMEM((comps, times, points), bf16),
            pltpu.VMEM((comps, times, points), bf16),
            table,
            table,
            spectra,
            spectra,
            half,
            half,
            half,
            half,
            half,
            half,
            pltpu.VMEM((FPG, comps, 4 * NBLK, points), bf16),
            pltpu.VMEM((STAGES, FPS, 8, 128), f32),
            pltpu.VMEM((STAGES, RED, 2, 8, 128), f32),
            pltpu.VMEM((STAGES, 2, 8, 128), f32),
            pltpu.VMEM((STAGES, ZS, 2, 8, 128), f32),
            pltpu.VMEM((STAGES, 2, 8, 128), f32),
            pltpu.VMEM((STAGES, CORES, 2, 8, 128), f32),
            dma((NB, comps)),
            dma((2,)),
            dma((STAGES, NB + 1)),
            dma((2,)),
            dma((2,)),
            dma((STAGES * NB, GRP)),
            dma((STAGES * NB, GRP)),
            dma((comps, GRP)),
            dma((comps, GRP)),
            dma((STAGES, RED)),
            dma((STAGES, RED)),
            dma((STAGES, ZS)),
            dma((STAGES, ZS)),
            dma((STAGES,)),
            dma((STAGES,)),
        ],
        compiler_params=pltpu.CompilerParams(
            collective_id=0, has_side_effects=True, vmem_limit_bytes=48 << 20
        ),
    )(*[pltpu.with_memory_space_constraint(a, pltpu.HBM) for a in (kept_bins, weights, snapshots)])
    return (jnp.transpose(modes, (0, 1, 3, 2, 4)), jnp.transpose(energies))


def solution(mesh):
    in_specs = (P(None, "grp", "sp"), P(), P("sp"))
    out_specs = (P(None, "grp", None, None, "sp"), P("grp", None))
    return jax.shard_map(shards, mesh=mesh, in_specs=in_specs, out_specs=out_specs, check_vma=False)
```

time: 91.4 us -> 87.6 us (0.958)
  Pallas kernels: 89.4 us -> 85.5 us
    pallas_call x1, Pallas kernels: 89.4 us -> 85.5 us  [shards(): pl.pallas_call(functools.partial(kernel, norm), out_shape=(jax.ShapeDtype...]
where the time goes in v3:
time: 87.6 us; the launch traced here: 87.4 us
  Pallas kernels  85.5 us (98%)
  local copies, waits for them, and re-layouts  1.29 us (1%)
    pallas_call x1, Pallas kernels, shards(): pl.pallas_call(functools.partial(kernel, norm), out_shape=(jax.ShapeDtype...  85.5 us

profile of v3, /device:TPU:1, one launch (start us, length us, event | category | flops | bytes accessed | tf_op | source)
XLA Modules:
  0.0 87.4 jit_solution(12518080464114004880)
XLA Ops:
  0.6 85.5 %shard_map.50 = (f32[2,8,3,4,384]{4,3,2,1,0:T(4,128)S(1)}, f32[4,8]{1,0:T(4,128)S(1)}) custom-call(s32[64]{0:T(128)} %bins_hbm.1, f32[384]{0:T(512)} %wts_hbm.1, f32[3,1024,384]{2,1,0:T(8,128)} %snap_ref.1), custom_call_target="tpu_custom_call" | custom-call | tf_op jit(solution)/shard_map/pallas_call | solution.py:493
  86.1 0.7 copy.7
  86.9 0.6 copy.8

commit v4 on v3

--- a/solution.py
+++ b/solution.py
@@ -84,7 +84,7 @@
     lengths = jnp.ones((1, w.shape[1]), jnp.float32)
     for m in range(MODES):
         length = jnp.sqrt(jnp.sum(left * left, axis=0, keepdims=True) + 1e-06)
-        unit = left / length
+        unit = left * (1.0 / length)
         basis = jnp.where(lane == m, unit, basis)
         lengths = jnp.where(lane_row == m, length, lengths)
         if m < MODES - 1:
@@ -125,14 +125,15 @@
 
 
 def subspace(embed):
+    e_hi = embed.astype(jnp.bfloat16).astype(jnp.float32)
+    e_both = e_hi + pltpu.roll(embed - e_hi, 64, 1)
+    left = jnp.concatenate([e_both, e_hi], axis=1).astype(jnp.bfloat16)
     w = embed
     for step in range(ITERS):
         basis, lengths = orthonormalize(w)
         if step < ITERS - 1:
-            padded = jnp.concatenate([basis, jnp.zeros_like(basis)], axis=0)
-            w = jnp.dot(
-                embed, padded, precision=lax.Precision.HIGHEST, preferred_element_type=jnp.float32
-            )
+            high, low = split(basis)
+            w = fdot(left, jnp.concatenate([high, high, low, jnp.zeros_like(low)], axis=0))
     scaled = basis * (1.0 / jnp.sqrt(NBLK * lengths))
     v_re, v_im = scaled[:NBLK], scaled[NBLK:]
     swapped = pltpu.roll(jnp.concatenate([v_im, v_re], axis=0), MODES, 1)
@@ -478,6 +479,17 @@
                 modes_ref[0, bin_at, c] = out[:MODES]
                 modes_ref[1, bin_at, c] = out[MODES:]
     en_ref[...] = energies[:MODES, :FPG]
+
+
+def copy_out(modes_ref, en_ref, modes_out, en_out, sem):
+    copies = [
+        pltpu.make_async_copy(modes_ref, modes_out, sem.at[0]),
+        pltpu.make_async_copy(en_ref, en_out, sem.at[1]),
+    ]
+    for copy in copies:
+        copy.start()
+    for copy in copies:
+        copy.wait()
 
 
 def shards(snapshots, kept_bins, weights):
@@ -541,6 +553,17 @@
             collective_id=0, has_side_effects=True, vmem_limit_bytes=48 << 20
         ),
     )(*[pltpu.with_memory_space_constraint(a, pltpu.HBM) for a in (kept_bins, weights, snapshots)])
+    modes, energies = pl.pallas_call(
+        copy_out,
+        out_shape=(
+            jax.ShapeDtypeStruct((2, FPG, comps, MODES, points), f32),
+            jax.ShapeDtypeStruct((MODES, FPG), f32),
+        ),
+        in_specs=[pl.BlockSpec(memory_space=pl.ANY)] * 2,
+        out_specs=(hbm, hbm),
+        scratch_shapes=[dma((2,))],
+        compiler_params=pltpu.CompilerParams(vmem_limit_bytes=4 << 20),
+    )(modes, energies)
     return (jnp.transpose(modes, (0, 1, 3, 2, 4)), jnp.transpose(energies))
 
 

time: 87.6 us -> 87 us (level)
  local copies, waits for them, and re-layouts: 1.29 us -> 0 us
    unnamed x2 -> x0, local copies, waits for them, and re-layouts: 1.29 us -> none
where the time goes in v4:
time: 87 us; the launch traced here: 86.8 us
  Pallas kernels  86.2 us (99%)
    pallas_call x1, Pallas kernels, shards(): pl.pallas_call(functools.partial(kernel, norm), out_shape=(jax.ShapeDtype...  85.5 us

profile of v4, /device:TPU:1, one launch (start us, length us, event | category | flops | bytes accessed | tf_op | source)
XLA Modules:
  0.0 86.8 jit_solution(15145182595106787256)
XLA Ops:
  0.6 85.5 %shard_map.50 = (f32[2,8,3,4,384]{4,3,2,1,0:T(4,128)S(1)}, f32[4,8]{1,0:T(4,128)S(1)}) custom-call(s32[64]{0:T(128)} %bins_hbm.1, f32[384]{0:T(512)} %wts_hbm.1, f32[3,1024,384]{2,1,0:T(8,128)} %snap_ref.1), custom_call_target="tpu_custom_call" | custom-call | tf_op jit(solution)/shard_map/pallas_call | solution.py:505
  86.1 0.7 shard_map.51

commit v5 on v4

--- a/solution.py
+++ b/solution.py
@@ -83,8 +83,10 @@
     basis = jnp.zeros_like(w)
     lengths = jnp.ones((1, w.shape[1]), jnp.float32)
     for m in range(MODES):
-        length = jnp.sqrt(jnp.sum(left * left, axis=0, keepdims=True) + 1e-06)
-        unit = left * (1.0 / length)
+        square = jnp.sum(left * left, axis=0, keepdims=True) + 1e-06
+        inverse = lax.rsqrt(square)
+        length = square * inverse
+        unit = left * inverse
         basis = jnp.where(lane == m, unit, basis)
         lengths = jnp.where(lane_row == m, length, lengths)
         if m < MODES - 1:

time: 87 us -> 86.9 us (level)
  no operation moved by 1% of the time
where the time goes in v5:
time: 86.9 us; the launch traced here: 86.7 us
  Pallas kernels  86.1 us (99%)
    pallas_call x1, Pallas kernels, shards(): pl.pallas_call(functools.partial(kernel, norm), out_shape=(jax.ShapeDtype...  85.4 us

profile of v5, /device:TPU:1, one launch (start us, length us, event | category | flops | bytes accessed | tf_op | source)
XLA Modules:
  0.0 86.7 jit_solution(8088254274164200632)
XLA Ops:
  0.6 85.4 %shard_map.50 = (f32[2,8,3,4,384]{4,3,2,1,0:T(4,128)S(1)}, f32[4,8]{1,0:T(4,128)S(1)}) custom-call(s32[64]{0:T(128)} %bins_hbm.1, f32[384]{0:T(512)} %wts_hbm.1, f32[3,1024,384]{2,1,0:T(8,128)} %snap_ref.1), custom_call_target="tpu_custom_call" | custom-call | tf_op jit(solution)/shard_map/pallas_call | solution.py:507
  86.0 0.7 shard_map.51
